TPU v7x, 32 devices: a whole 2x2x4 slice. The times are simulated.
32 devices in a mesh: depth: 16 (over z, x, core), band: 2 (over y).
Axes of the slice: x: 2, y: 2, z: 4, core: 2. Of those that a mesh axis runs over, the one named last changes fastest.
Arguments:
- volume: int32 [64, 64, 1024], P('depth', 'band'), may hold values from 0 to 255
- tf_table: int32 [4, 256], replicated, may hold values from 0 to 255
- view_code: int32 [2, 4], replicated, may hold values from -20 to 20
Outputs:
- final_image: float32 [2, 1024, 4, 64], P(None, 'depth', None, 'band')
All inputs are finite; a program needn't handle non-finite values.
Results may differ from a plain program's by a relative error of at most 0.0014.
Values may be sent and summed in bfloat16 or wider, within the bound.
A program may use at most 64 MiB of HBM per device.

v0:
```python
import math
import jax
import jax.numpy as jnp
from jax import lax
from jax.sharding import PartitionSpec as P

VIEWS = 2
MARGIN = 16


def extended(x, sides, width):
    for axis, dim in sides:
        size, length = (lax.axis_size(axis), x.shape[dim])
        up = [(i, (i + 1) % size) for i in range(size - 1)]
        down = [(j, i) for i, j in up]
        last = lax.slice_in_dim(x, length - width, length, axis=dim)
        first = lax.slice_in_dim(x, 0, width, axis=dim)
        before = lax.ppermute(last, axis, up)
        after = lax.ppermute(first, axis, down)
        x = jnp.concatenate([before, x, after], axis=dim)
    return x


def lanczos(offset):
    return jnp.where(jnp.abs(offset) < 3.0, jnp.sinc(offset) * jnp.sinc(offset / 3.0), 0.0)


def split_offset(coefficient, position, length, lift=0):
    numerator = coefficient * (2 * position + 1 - length) + lift * length
    integer_part = numerator // (2 * length)
    fraction = (numerator - integer_part * (2 * length)).astype(jnp.float32) / (2.0 * length)
    return (integer_part, fraction)


def make_palette(tf_table, depth_count):
    table_float = tf_table.astype(jnp.float32)
    opacity = table_float[3] / (64.0 * depth_count)
    premult = table_float[0:3] / 255.0 * opacity
    return jnp.concatenate([premult, opacity[None]], axis=0).astype(jnp.bfloat16)


def classify(codes, palette):
    shape = codes.shape
    last = shape[-1]
    rows = codes.reshape(-1, last)
    row_count = rows.shape[0]
    group_rows = math.gcd(row_count, 8)
    grouped = rows.reshape(row_count // group_rows, group_rows, last)
    table = palette.reshape(4, 16, 16)
    levels = jnp.arange(16, dtype=jnp.int32)

    def lookup(block_codes):
        high_part = block_codes // 16
        low_part = block_codes - high_part * 16
        low_hot = (low_part[None] == levels[:, None, None]).astype(jnp.bfloat16)
        partial_value = jnp.einsum(
            "chl,lgk->chgk", table, low_hot, preferred_element_type=jnp.float32
        )
        high_hot = (high_part[None] == levels[:, None, None]).astype(jnp.float32)
        return jnp.sum(partial_value * high_hot[None], axis=1)

    picked = lax.map(lookup, grouped)
    picked = jnp.transpose(picked, (1, 0, 2, 3)).reshape((4,) + shape)
    return picked.astype(jnp.bfloat16)


def column_weights(integer_part, fraction, block):
    inputs = jnp.arange(3 * block, dtype=jnp.int32)[:, None]
    outputs = jnp.arange(block, dtype=jnp.int32)[None, :]
    distance = inputs - block - outputs - integer_part
    return lanczos(fraction - distance.astype(jnp.float32)).astype(jnp.bfloat16)


def row_weights(integer_part, fraction, out_rows, in_rows, margin):
    outputs = jnp.arange(out_rows, dtype=jnp.int32)[:, None]
    inputs = jnp.arange(in_rows, dtype=jnp.int32)[None, :]
    distance = inputs - margin - outputs - integer_part
    return lanczos(fraction - distance.astype(jnp.float32)).astype(jnp.bfloat16)


def warp_weights(coefficient, first_column, strip_width, margin, total_width):
    columns = first_column + jnp.arange(strip_width, dtype=jnp.int32)
    integer_part, fraction = split_offset(coefficient, columns, total_width, 1)
    inputs = jnp.arange(strip_width + 2 * margin, dtype=jnp.int32)[None, :]
    outputs = jnp.arange(strip_width, dtype=jnp.int32)[:, None]
    distance = inputs - margin - outputs - integer_part[:, None]
    return lanczos(fraction[:, None] - distance.astype(jnp.float32))


def shear_columns(source, tap_matrix, block):
    channels, row_count, extent = source.shape
    blocks = extent // block
    padded = jnp.pad(source, ((0, 0), (0, 0), (block, block)))
    tile_view = padded.reshape(channels, row_count, blocks + 2, block)
    windows = jnp.concatenate(
        [
            tile_view[:, :, 0:blocks],
            tile_view[:, :, 1 : blocks + 1],
            tile_view[:, :, 2 : blocks + 2],
        ],
        axis=3,
    )
    result = jnp.einsum("crbk,kj->bjcr", windows, tap_matrix, preferred_element_type=jnp.float32)
    return result.reshape(extent, channels, row_count).astype(jnp.bfloat16)


def shear_rows(source, tap_matrix):
    return jnp.einsum("xcr,yr->xcy", source, tap_matrix, preferred_element_type=jnp.float32)


def over(front_part, back_part):
    return front_part + (1.0 - front_part[..., 3:4, :]) * back_part


def body(volume, tf_table, view_code):
    slab_count, band_rows, extent = volume.shape
    depth_size = lax.axis_size("depth")
    depth_rank = lax.axis_index("depth")
    total_depth = slab_count * depth_size
    block = min(128, extent)
    strip_width = extent // depth_size
    widened_rows = band_rows + 2 * MARGIN
    palette = make_palette(tf_table, total_depth)
    classified = classify(volume, palette)
    widened = extended(classified, (("band", 2),), MARGIN)
    finals = []
    for view_index in range(VIEWS):
        params = view_code[view_index]
        facing = params[3] >= 0
        picture = jnp.zeros((extent, 4, band_rows), jnp.float32)
        for step_index in range(slab_count):
            local_slice = jnp.where(facing, step_index, slab_count - 1 - step_index).astype(
                jnp.int32
            )
            global_slice = depth_rank * slab_count + local_slice
            whole_y, frac_y = split_offset(params[1], global_slice, total_depth)
            whole_x, frac_x = split_offset(params[0], global_slice, total_depth)
            current = lax.dynamic_index_in_dim(widened, local_slice, 1, keepdims=False)
            row_sheared = shear_columns(current, column_weights(whole_x, frac_x, block), block)
            sheared = shear_rows(
                row_sheared, row_weights(whole_y, frac_y, band_rows, widened_rows, MARGIN)
            )
            picture = over(picture, sheared)
        pieces = picture.reshape(depth_size, strip_width, 4, band_rows)
        arrived = lax.all_to_all(
            pieces.astype(jnp.bfloat16), "depth", split_axis=0, concat_axis=0, tiled=True
        ).astype(pieces.dtype)
        for level_index in range(depth_size.bit_length() - 1):
            paired = arrived.reshape((arrived.shape[0] // 2, 2) + arrived.shape[1:])
            earlier = paired[:, 0]
            later = paired[:, 1]
            front_part = jnp.where(facing, earlier, later)
            back_part = jnp.where(facing, later, earlier)
            arrived = over(front_part, back_part)
        strip = arrived[0]
        padded_strip = extended(strip, (("depth", 0),), MARGIN)
        weights = warp_weights(params[2], depth_rank * strip_width, strip_width, MARGIN, extent)
        final_strip = jnp.einsum(
            "ck,kay->cay",
            weights,
            padded_strip,
            precision=lax.Precision.HIGHEST,
            preferred_element_type=jnp.float32,
        )
        finals.append(final_strip)
    return jnp.stack(finals)


def solution(mesh):
    placed = (P("depth", "band", None), P(), P())
    return jax.shard_map(
        body, mesh=mesh, in_specs=placed, out_specs=P(None, "depth", None, "band"), check_vma=False
    )
```

profile of v0, /device:TPU:8, one launch (start us, length us, event | category | flops | bytes accessed | tf_op | source)
XLA Modules:
  0.0 122.0 jit_solution(5489275752223972056)
XLA Ops:
  0.9 24.4 %while.14 = (s32[]{:T(128)}, bf16[16,4,8,1024]{3,2,0,1:T(8,128)(2,1)S(1)}, s32[16,8,1024]{2,1,0:T(8,128)}, bf16[4,16,16]{2,1,0:T(8,128)(2,1)S(1)}, s32[]{:T(128)}) while((s32[]{:T(128)}, bf16[16,4,8,1024]{3,2,0,1:T(8,128)(2,1)S(1)}, s32[16,8,1024]{2,1,0:T(8,128)}, bf16[4,16,16]{2,1,0:T(8,128)(2,1)S(1)}, s32[]{:T(128)}) %tuple.78), condition=%wide.region_2.5_spmd.clone.clone, body=%wide.region_0.4_spmd.clone.clone.sunk | while | flops 18325504 | bytes 1411149 | solution.py:62
  25.5 1.3 %collective-permute-start.1 = (bf16[4,4,16,1024]{3,2,1,0:T(8,128)(2,1)S(1)}, bf16[4,4,16,1024]{3,2,1,0:T(8,128)(2,1)S(1)}, u32[]{:S(2)}, u32[]{:S(2)}) collective-permute-start(bf16[4,4,16,1024]{3,2,1,0:T(8,128)(2,1)S(1)} %get-tuple-element.149), channel_id=1, source_target_pairs={{1,0},{3,2},{5,4},{7,6},{9,8},{11,10},{13,12},{15,14},{17,16},{19,... | collective-permute-start | bytes 1572872 | tf_op jit(solution)/shard_map/ppermute | solution.py:19
  26.8 4.6 %collective-permute-start = (bf16[4,4,16,1024]{3,2,1,0:T(8,128)(2,1)S(1)}, bf16[4,4,16,1024]{3,2,1,0:T(8,128)(2,1)S(1)}, u32[]{:S(2)}, u32[]{:S(2)}) collective-permute-start(bf16[4,4,16,1024]{3,2,1,0:T(8,128)(2,1)S(1)} %get-tuple-element.148), channel_id=1, source_target_pairs={{0,1},{2,3},{4,5},{6,7},{8,9},{10,11},{12,13},{14,15},{16,17},{18,... | collective-permute-start | bytes 1572872 | tf_op jit(solution)/shard_map/ppermute | solution.py:18
  43.9 1.2 and_select_fusion
  45.1 1.2 convert_multiply_fusion
  48.5 1.7 %dynamic-slice_bitcast_fusion.4 = (bf16[4,64,1024]{2,1,0:T(8,128)(2,1)S(1)}, bf16[4,64,1024]{2,1,0:T(8,128)(2,1)}, bf16[4,64,1024]{2,1,0:T(8,128)(2,1)}, bf16[4,...) fusion(bf16[4,4,64,1024]{3,2,1,0:T(8,128)(2,1)S(1)} %pad_maximu, ...), kind=kLoop, calls=%fused_computation.126 | loop fusion | bytes 8388640 | tf_op jit(solution)/shard_map/jit(dynamic_index_in_dim)/squeeze | solution.py:138
  51.1 0.9 copy.254
  52.0 0.9 copy.253
  56.5 1.1 fusion.95
  59.6 0.9 copy.260
  60.5 0.9 copy.259
  61.5 1.1 fusion.98
  65.7 1.1 fusion.101
  67.0 1.1 fusion.104
  68.9 1.1 reshape.474
  70.0 6.3 %all-to-all-start.1 = ((bf16[16,2,4096]{2,1,0:T(2,128)(2,1)}), bf16[16,2,4096]{2,1,0:T(2,128)(2,1)S(1)}, u32[]{:S(2)}, u32[]{:S(2)}) async-start(bf16[16,2,4096]{2,1,0:T(2,128)(2,1)} %reshape.474), calls=%async_computation.1 | async-start | bytes 524288 | tf_op jit(solution)/shard_map/all_to_all | solution.py:145
  79.8 0.9 copy.246
  80.7 0.9 copy.245
  81.6 0.9 copy.244
  82.6 1.1 fusion.83
  85.5 0.9 copy.248
  87.3 1.1 fusion.86
  91.3 1.1 fusion.89
  92.4 1.1 fusion.92
  94.5 1.1 reshape.476
  95.6 6.0 %all-to-all-start = ((bf16[16,2,4096]{2,1,0:T(2,128)(2,1)}), bf16[16,2,4096]{2,1,0:T(2,128)(2,1)S(1)}, u32[]{:S(2)}, u32[]{:S(2)}) async-start(bf16[16,2,4096]{2,1,0:T(2,128)(2,1)} %reshape.476), calls=%async_computation | async-start | bytes 524288 | tf_op jit(solution)/shard_map/all_to_all | solution.py:145
  102.7 3.1 %collective-permute-start.5 = (f32[16,4,32]{0,2,1:T(8,128)S(1)}, f32[16,4,32]{0,2,1:T(8,128)S(1)}, u32[]{:S(2)}, u32[]{:S(2)}) collective-permute-start(f32[16,4,32]{0,2,1:T(8,128)S(1)} %get-tuple-element.157), channel_id=1, source_target_pairs={{2,0},{4,2},{6,4},{8,6},{10,8},{12,10},{14,12},{16,14},{18,16},{20... | collective-permute-start | bytes 24584 | tf_op jit(solution)/shard_map/ppermute | solution.py:19
  105.8 1.9 %collective-permute-start.4 = (f32[16,4,32]{0,2,1:T(8,128)S(1)}, f32[16,4,32]{0,2,1:T(8,128)S(1)}, u32[]{:S(2)}, u32[]{:S(2)}) collective-permute-start(f32[16,4,32]{0,2,1:T(8,128)S(1)} %get-tuple-element.156), channel_id=1, source_target_pairs={{0,2},{2,4},{4,6},{6,8},{8,10},{10,12},{12,14},{14,16},{16,18},{18... | collective-permute-start | bytes 24584 | tf_op jit(solution)/shard_map/ppermute | solution.py:18
  107.7 1.5 %all-to-all-done = bf16[16,2,4096]{2,1,0:T(2,128)(2,1)S(1)} async-done(((bf16[16,2,4096]{2,1,0:T(2,128)(2,1)}), bf16[16,2,4096]{2,1,0:T(2,128)(2,1)S(1)}, u32[]{:S(2)}, u32[]{:S(2)}) %all-to-all-start) | async-done | bytes 262176 | tf_op jit(solution)/shard_map/all_to_all | solution.py:145
  110.3 4.0 %collective-permute-start.3 = (f32[16,4,32]{0,2,1:T(8,128)S(1)}, f32[16,4,32]{0,2,1:T(8,128)S(1)}, u32[]{:S(2)}, u32[]{:S(2)}) collective-permute-start(f32[16,4,32]{0,2,1:T(8,128)S(1)} %get-tuple-element.155), channel_id=1, source_target_pairs={{2,0},{4,2},{6,4},{8,6},{10,8},{12,10},{14,12},{16,14},{18,16},{20... | collective-permute-start | bytes 24584 | tf_op jit(solution)/shard_map/ppermute | solution.py:19
  114.3 1.9 %collective-permute-start.2 = (f32[16,4,32]{0,2,1:T(8,128)S(1)}, f32[16,4,32]{0,2,1:T(8,128)S(1)}, u32[]{:S(2)}, u32[]{:S(2)}) collective-permute-start(f32[16,4,32]{0,2,1:T(8,128)S(1)} %get-tuple-element.154), channel_id=1, source_target_pairs={{0,2},{2,4},{4,6},{6,8},{8,10},{10,12},{12,14},{14,16},{16,18},{18... | collective-permute-start | bytes 24584 | tf_op jit(solution)/shard_map/ppermute | solution.py:18
  116.8 4.0 %collective-permute-done.2 = f32[16,4,32]{0,2,1:T(8,128)S(1)} collective-permute-done((f32[16,4,32]{0,2,1:T(8,128)S(1)}, f32[16,4,32]{0,2,1:T(8,128)S(1)}, u32[]{:S(2)}, u32[]{:S(2)}) %collective-permute-start.2) | collective-permute-done | bytes 8224 | tf_op jit(solution)/shard_map/ppermute | solution.py:18
  (233 shorter events, 51.6 us)
Async XLA Ops:
  25.3 6.0 %copy-start.22 = (s32[2,4]{1,0:T(2,128)S(1)}, s32[2,4]{1,0:T(2,128)}, u32[]{:S(2)}) copy-start(s32[2,4]{1,0:T(2,128)} %param.10) | copy-start | bytes 100
  25.5 22.7 %collective-permute-start.1 = (bf16[4,4,16,1024]{3,2,1,0:T(8,128)(2,1)S(1)}, bf16[4,4,16,1024]{3,2,1,0:T(8,128)(2,1)S(1)}, u32[]{:S(2)}, u32[]{:S(2)}) collective-permute-start(bf16[4,4,16,1024]{3,2,1,0:T(8,128)(2,1)S(1)} %get-tuple-element.149), channel_id=1, source_target_pairs={{1,0},{3,2},{5,4},{7,6},{9,8},{11,10},{13,12},{15,14},{17,16},{19,... | collective-permute-start | bytes 1572872 | tf_op jit(solution)/shard_map/ppermute | solution.py:19
  26.8 21.4 %collective-permute-start = (bf16[4,4,16,1024]{3,2,1,0:T(8,128)(2,1)S(1)}, bf16[4,4,16,1024]{3,2,1,0:T(8,128)(2,1)S(1)}, u32[]{:S(2)}, u32[]{:S(2)}) collective-permute-start(bf16[4,4,16,1024]{3,2,1,0:T(8,128)(2,1)S(1)} %get-tuple-element.148), channel_id=1, source_target_pairs={{0,1},{2,3},{4,5},{6,7},{8,9},{10,11},{12,13},{14,15},{16,17},{18,... | collective-permute-start | bytes 1572872 | tf_op jit(solution)/shard_map/ppermute | solution.py:18
  53.7 2.8 %copy-start.16 = (bf16[4,64,8,128]{3,1,2,0:T(8,128)(2,1)S(1)}, bf16[4,64,8,128]{3,1,2,0:T(8,128)(2,1)}, u32[]{:S(2)}) copy-start(bf16[4,64,8,128]{3,1,2,0:T(8,128)(2,1)} %copy.254) | copy-start | bytes 1572868
  53.7 2.8 %copy-start.18 = (bf16[4,64,8,128]{3,1,2,0:T(8,128)(2,1)S(1)}, bf16[4,64,8,128]{3,1,2,0:T(8,128)(2,1)}, u32[]{:S(2)}) copy-start(bf16[4,64,8,128]{3,1,2,0:T(8,128)(2,1)} %copy.253) | copy-start | bytes 1572868
  56.5 1.3 %copy-start.4 = (bf16[4,64,1024]{2,1,0:T(8,128)(2,1)S(1)}, bf16[4,64,1024]{2,1,0:T(8,128)(2,1)}, u32[]{:S(2)}) copy-start(bf16[4,64,1024]{2,1,0:T(8,128)(2,1)} %get-tuple-element.114) | copy-start | bytes 1572868
  58.6 2.8 %copy-start.9 = (bf16[4,64,8,128]{3,1,2,0:T(8,128)(2,1)S(1)}, bf16[4,64,8,128]{3,1,2,0:T(8,128)(2,1)}, u32[]{:S(2)}) copy-start(bf16[4,64,8,128]{3,1,2,0:T(8,128)(2,1)} %copy.258) | copy-start | bytes 1572868
  58.6 2.8 %copy-start.11 = (bf16[4,64,8,128]{3,1,2,0:T(8,128)(2,1)S(1)}, bf16[4,64,8,128]{3,1,2,0:T(8,128)(2,1)}, u32[]{:S(2)}) copy-start(bf16[4,64,8,128]{3,1,2,0:T(8,128)(2,1)} %copy.257) | copy-start | bytes 1572868
  58.6 2.8 %copy-start.14 = (bf16[4,64,8,128]{3,1,2,0:T(8,128)(2,1)S(1)}, bf16[4,64,8,128]{3,1,2,0:T(8,128)(2,1)}, u32[]{:S(2)}) copy-start(bf16[4,64,8,128]{3,1,2,0:T(8,128)(2,1)} %copy.256) | copy-start | bytes 1572868
  62.5 1.0 copy-start.3
  64.3 1.2 copy-start.7
  64.3 1.3 %copy-start.12 = (bf16[4,64,8,128]{3,1,2,0:T(8,128)(2,1)S(1)}, bf16[4,64,8,128]{3,1,2,0:T(8,128)(2,1)}, u32[]{:S(2)}) copy-start(bf16[4,64,8,128]{3,1,2,0:T(8,128)(2,1)} %copy.259) | copy-start | bytes 1572868
  68.1 8.1 %copy-start.2 = (bf16[4,64,1024]{2,1,0:T(8,128)(2,1)S(1)}, bf16[4,64,1024]{2,1,0:T(8,128)(2,1)}, u32[]{:S(2)}) copy-start(bf16[4,64,1024]{2,1,0:T(8,128)(2,1)} %get-tuple-element.119) | copy-start | bytes 1572868
  70.0 25.6 %all-to-all-start.1 = ((bf16[16,2,4096]{2,1,0:T(2,128)(2,1)}), bf16[16,2,4096]{2,1,0:T(2,128)(2,1)S(1)}, u32[]{:S(2)}, u32[]{:S(2)}) async-start(bf16[16,2,4096]{2,1,0:T(2,128)(2,1)} %reshape.474), calls=%async_computation.1 | async-start | bytes 524288 | tf_op jit(solution)/shard_map/all_to_all | solution.py:145
  77.0 2.0 %copy-start.1 = (bf16[4,64,1024]{2,1,0:T(8,128)(2,1)S(1)}, bf16[4,64,1024]{2,1,0:T(8,128)(2,1)}, u32[]{:S(2)}) copy-start(bf16[4,64,1024]{2,1,0:T(8,128)(2,1)} %get-tuple-element.118) | copy-start | bytes 1572868
  79.7 2.8 %copy-start.17 = (bf16[4,64,8,128]{3,1,2,0:T(8,128)(2,1)S(1)}, bf16[4,64,8,128]{3,1,2,0:T(8,128)(2,1)}, u32[]{:S(2)}) copy-start(bf16[4,64,8,128]{3,1,2,0:T(8,128)(2,1)} %copy.242) | copy-start | bytes 1572868
  79.7 2.8 %copy-start.19 = (bf16[4,64,8,128]{3,1,2,0:T(8,128)(2,1)S(1)}, bf16[4,64,8,128]{3,1,2,0:T(8,128)(2,1)}, u32[]{:S(2)}) copy-start(bf16[4,64,8,128]{3,1,2,0:T(8,128)(2,1)} %copy.241) | copy-start | bytes 1572868
  82.6 2.0 %copy-start = (bf16[4,64,1024]{2,1,0:T(8,128)(2,1)S(1)}, bf16[4,64,1024]{2,1,0:T(8,128)(2,1)}, u32[]{:S(2)}) copy-start(bf16[4,64,1024]{2,1,0:T(8,128)(2,1)} %get-tuple-element.117) | copy-start | bytes 1572868
  85.3 2.0 %copy-start.10 = (bf16[4,64,8,128]{3,1,2,0:T(8,128)(2,1)S(1)}, bf16[4,64,8,128]{3,1,2,0:T(8,128)(2,1)}, u32[]{:S(2)}) copy-start(bf16[4,64,8,128]{3,1,2,0:T(8,128)(2,1)} %copy.246) | copy-start | bytes 1572868
  85.3 2.0 %copy-start.13 = (bf16[4,64,8,128]{3,1,2,0:T(8,128)(2,1)S(1)}, bf16[4,64,8,128]{3,1,2,0:T(8,128)(2,1)}, u32[]{:S(2)}) copy-start(bf16[4,64,8,128]{3,1,2,0:T(8,128)(2,1)} %copy.245) | copy-start | bytes 1572868
  85.3 2.0 %copy-start.15 = (bf16[4,64,8,128]{3,1,2,0:T(8,128)(2,1)S(1)}, bf16[4,64,8,128]{3,1,2,0:T(8,128)(2,1)}, u32[]{:S(2)}) copy-start(bf16[4,64,8,128]{3,1,2,0:T(8,128)(2,1)} %copy.244) | copy-start | bytes 1572868
  87.3 1.1 copy-start.21
  90.1 1.2 copy-start.8
  92.4 1.1 copy-start.20
  95.6 13.6 %all-to-all-start = ((bf16[16,2,4096]{2,1,0:T(2,128)(2,1)}), bf16[16,2,4096]{2,1,0:T(2,128)(2,1)S(1)}, u32[]{:S(2)}, u32[]{:S(2)}) async-start(bf16[16,2,4096]{2,1,0:T(2,128)(2,1)} %reshape.476), calls=%async_computation | async-start | bytes 524288 | tf_op jit(solution)/shard_map/all_to_all | solution.py:145
  102.7 13.6 %collective-permute-start.5 = (f32[16,4,32]{0,2,1:T(8,128)S(1)}, f32[16,4,32]{0,2,1:T(8,128)S(1)}, u32[]{:S(2)}, u32[]{:S(2)}) collective-permute-start(f32[16,4,32]{0,2,1:T(8,128)S(1)} %get-tuple-element.157), channel_id=1, source_target_pairs={{2,0},{4,2},{6,4},{8,6},{10,8},{12,10},{14,12},{16,14},{18,16},{20... | collective-permute-start | bytes 24584 | tf_op jit(solution)/shard_map/ppermute | solution.py:19
  105.8 10.5 %collective-permute-start.4 = (f32[16,4,32]{0,2,1:T(8,128)S(1)}, f32[16,4,32]{0,2,1:T(8,128)S(1)}, u32[]{:S(2)}, u32[]{:S(2)}) collective-permute-start(f32[16,4,32]{0,2,1:T(8,128)S(1)} %get-tuple-element.156), channel_id=1, source_target_pairs={{0,2},{2,4},{4,6},{6,8},{8,10},{10,12},{12,14},{14,16},{16,18},{18... | collective-permute-start | bytes 24584 | tf_op jit(solution)/shard_map/ppermute | solution.py:18
  109.9 6.5 %copy-start.23 = (s32[64]{0:T(128)S(1)}, s32[64]{0:T(128)}, u32[]{:S(2)}) copy-start(s32[64]{0:T(128)} %and_select_fusion) | copy-start | bytes 772
  109.9 6.5 %copy-start.24 = (f32[64]{0:T(128)S(1)}, f32[64]{0:T(128)}, u32[]{:S(2)}) copy-start(f32[64]{0:T(128)} %convert_multiply_fusion) | copy-start | bytes 772
  109.9 6.5 %copy-start.25 = (s32[96]{0:T(128)S(1)}, s32[96]{0:T(128)}, u32[]{:S(2)}) copy-start(s32[96]{0:T(128)} %iota_add_fusion.2) | copy-start | bytes 1156
  110.3 6.5 %collective-permute-start.3 = (f32[16,4,32]{0,2,1:T(8,128)S(1)}, f32[16,4,32]{0,2,1:T(8,128)S(1)}, u32[]{:S(2)}, u32[]{:S(2)}) collective-permute-start(f32[16,4,32]{0,2,1:T(8,128)S(1)} %get-tuple-element.155), channel_id=1, source_target_pairs={{2,0},{4,2},{6,4},{8,6},{10,8},{12,10},{14,12},{16,14},{18,16},{20... | collective-permute-start | bytes 24584 | tf_op jit(solution)/shard_map/ppermute | solution.py:19
  114.3 6.5 %collective-permute-start.2 = (f32[16,4,32]{0,2,1:T(8,128)S(1)}, f32[16,4,32]{0,2,1:T(8,128)S(1)}, u32[]{:S(2)}, u32[]{:S(2)}) collective-permute-start(f32[16,4,32]{0,2,1:T(8,128)S(1)} %get-tuple-element.154), channel_id=1, source_target_pairs={{0,2},{2,4},{4,6},{6,8},{8,10},{10,12},{12,14},{14,16},{16,18},{18... | collective-permute-start | bytes 24584 | tf_op jit(solution)/shard_map/ppermute | solution.py:18
  (2 other events, 2.1 us)
where the time goes:
time: 124 us; the launch traced here: 122 us
  local copies, waits for them, and re-layouts  30.6 us (25%)
  starting transfers between devices  29.1 us (23%)
  other arithmetic  22 us (18%)
  matrix products  21.2 us (17%)
  between operations  12.9 us (10%)
  waiting for transfers between devices  5.49 us (4%)
    unnamed x80, local copies, waits for them, and re-layouts  20.5 us
    eq x16, other arithmetic, lookup(): low_hot = (low_part[None] == levels[:, None, None]).astype(jnp.bfloat16)  12.6 us
    all_to_all x2, starting transfers between devices, body(): lax.all_to_all(pieces.astype(jnp.bfloat16), 'depth', split_axis=0, concat...  12.3 us
    dot_general x16, matrix products, lookup(): jnp.einsum('chl,lgk->chgk', table, low_hot, preferred_element_type=jnp.fl...  10.1 us
    dot_general x8, matrix products, shear_columns(): jnp.einsum('crbk,kj->bjcr', windows, tap_matrix, preferred_element_type=j...  8.45 us
    ppermute x3, starting transfers between devices, extended(): before = lax.ppermute(last, axis, up)  8.45 us
    ppermute x3, starting transfers between devices, extended(): after = lax.ppermute(first, axis, down)  8.41 us
    ppermute x3, waiting for transfers between devices, extended(): before = lax.ppermute(last, axis, up)  4.03 us
  transfers between devices with their start and end apart: 8, of which 2 were waited for; matrix products, arithmetic and copies ran while one was open for 21% of the time, Pallas kernels for 0%

commit v1 on v0

--- a/solution.py
+++ b/solution.py
@@ -6,6 +6,29 @@
 
 VIEWS = 2
 MARGIN = 16
+
+
+def in_blocks(x, dim, length):
+    lengths = x.shape
+    pieces = x.reshape(*lengths[:dim], length, lengths[dim] // length, *lengths[dim + 1 :])
+    return jnp.moveaxis(pieces, dim, 0)
+
+
+def joined_along(blocks, dim):
+    shape = list(blocks.shape[1:])
+    shape[dim] *= blocks.shape[0]
+    return jnp.moveaxis(blocks, 0, dim).reshape(shape)
+
+
+def rotated_exchange(shard, axis, split_dim, concat_dim):
+    size, mine = (lax.axis_size(axis), lax.axis_index(axis))
+    blocks = in_blocks(shard, split_dim, size)
+    gathered = [blocks[mine]]
+    for step in range(1, size):
+        sent = blocks[(mine + step) % size]
+        gathered.append(lax.ppermute(sent, axis, [(i, (i + step) % size) for i in range(size)]))
+    blocks = jnp.stack(gathered)[(mine - jnp.arange(size)) % size]
+    return joined_along(blocks, concat_dim)
 
 
 def extended(x, sides, width):
@@ -142,9 +165,7 @@
             )
             picture = over(picture, sheared)
         pieces = picture.reshape(depth_size, strip_width, 4, band_rows)
-        arrived = lax.all_to_all(
-            pieces.astype(jnp.bfloat16), "depth", split_axis=0, concat_axis=0, tiled=True
-        ).astype(pieces.dtype)
+        arrived = rotated_exchange(pieces.astype(jnp.bfloat16), "depth", 0, 0).astype(pieces.dtype)
         for level_index in range(depth_size.bit_length() - 1):
             paired = arrived.reshape((arrived.shape[0] // 2, 2) + arrived.shape[1:])
             earlier = paired[:, 0]

time: 124 us -> 155 us (1.25)
  starting transfers between devices: 29.1 us -> 60.4 us
  local copies, waits for them, and re-layouts: 30.6 us -> 34.1 us
  other arithmetic: 22 us -> 19 us
    ppermute x0 -> x30, starting transfers between devices: none -> 44.2 us  [rotated_exchange(): lax.ppermute(sent, axis, [(i, (i + step) % size) for i in range(size)])]
    all_to_all x2 -> x0, starting transfers between devices: 12.3 us -> none  [body(): lax.all_to_all(pieces.astype(jnp.bfloat16), 'depth', split_axis=0, concat...]
    squeeze x0 -> x1, local copies, waits for them, and re-layouts: none -> 3.75 us  [rotated_exchange(): sent = blocks[(mine + step) % size]]
    unnamed x80 -> x126, local copies, waits for them, and re-layouts: 20.5 us -> 19 us
  transfers between devices with their start and end apart: 8 -> 36, of which waited for: 2 -> 1; matrix products, arithmetic and copies ran while one was open for 21% -> 4% of each run, Pallas kernels for 0% -> 0%
where the time goes in v1:
time: 155 us; the launch traced here: 153 us
  starting transfers between devices  60.4 us (39%)
  local copies, waits for them, and re-layouts  34.1 us (22%)
  matrix products  21.2 us (14%)
  other arithmetic  19 us (12%)
  between operations  13.6 us (9%)
  waiting for transfers between devices  4.14 us (3%)
    ppermute x30, starting transfers between devices, rotated_exchange(): lax.ppermute(sent, axis, [(i, (i + step) % size) for i in range(size)])  44.2 us
    unnamed x126, local copies, waits for them, and re-layouts  19 us
    eq x16, other arithmetic, lookup(): low_hot = (low_part[None] == levels[:, None, None]).astype(jnp.bfloat16)  12.6 us
    dot_general x16, matrix products, lookup(): jnp.einsum('chl,lgk->chgk', table, low_hot, preferred_element_type=jnp.fl...  10.1 us
    ppermute x3, starting transfers between devices, extended(): before = lax.ppermute(last, axis, up)  8.92 us
    dot_general x8, matrix products, shear_columns(): jnp.einsum('crbk,kj->bjcr', windows, tap_matrix, preferred_element_type=j...  8.45 us
    ppermute x3, starting transfers between devices, extended(): after = lax.ppermute(first, axis, down)  7.3 us
    ppermute x3, waiting for transfers between devices, extended(): before = lax.ppermute(last, axis, up)  4.06 us
  transfers between devices with their start and end apart: 36, of which 1 were waited for; matrix products, arithmetic and copies ran while one was open for 4% of the time, Pallas kernels for 0%

profile of v1, /device:TPU:8, one launch (start us, length us, event | category | flops | bytes accessed | tf_op | source)
XLA Modules:
  0.0 153.2 jit_solution(16823028119471408063)
XLA Ops:
  0.9 24.4 %while.14 = (s32[]{:T(128)}, bf16[16,4,8,1024]{3,2,0,1:T(8,128)(2,1)S(1)}, s32[16,8,1024]{2,1,0:T(8,128)}, bf16[4,16,16]{2,1,0:T(8,128)(2,1)S(1)}, s32[]{:T(128)}) while((s32[]{:T(128)}, bf16[16,4,8,1024]{3,2,0,1:T(8,128)(2,1)S(1)}, s32[16,8,1024]{2,1,0:T(8,128)}, bf16[4,16,16]{2,1,0:T(8,128)(2,1)S(1)}, ...), condition=%wide.region_2.5_spmd.clone.clone, body=%wide.region_0.4_spmd.clone.clone.sunk | while | flops 18325504 | bytes 1411149 | solution.py:85
  25.5 1.3 collective-permute-start.1
  26.8 4.6 %collective-permute-start = (bf16[4,4,16,1024]{3,2,1,0:T(8,128)(2,1)S(1)}, bf16[4,4,16,1024]{3,2,1,0:T(8,128)(2,1)S(1)}, u32[]{:S(2)}, u32[]{:S(2)}) collective-permute-start(bf16[4,4,16,1024]{3,2,1,0:T(8,128)(2,1)S(1)} %get-tuple-element.148), channel_id=1, source_target_pairs={{0,1},{2,3},{4,5},{6,7},{8,9},{10,11},{12,13},{14,15},{16,17},{18,... | collective-permute-start | bytes 1572872 | tf_op jit(solution)/shard_map/ppermute | solution.py:41
  47.1 1.7 %dynamic-slice_bitcast_fusion.4 = (bf16[4,64,1024]{2,1,0:T(8,128)(2,1)}, bf16[4,64,1024]{2,1,0:T(8,128)(2,1)}, bf16[4,64,1024]{2,1,0:T(8,128)(2,1)}, bf16[4,64,1...) fusion(bf16[4,4,64,1024]{3,2,1,0:T(8,128)(2,1)S(1)} %pad_maximu, ...), kind=kLoop, calls=%fused_computation.127 | loop fusion | bytes 8388640 | tf_op jit(solution)/shard_map/jit(dynamic_index_in_dim)/squeeze | solution.py:161
  55.1 1.1 fusion.95
  65.6 1.1 fusion.104
  85.3 3.7 %constant_dynamic-slice_fusion = (bf16[1,64,4,32]{1,0,3,2:T(2,128)(2,1)S(1)}, bf16[1,64,4,32]{1,0,3,2:T(2,128)(2,1)S(1)}, bf16[1,64,4,32]{1,0,3,2:T(2,128)(2,1)S...) fusion(bf16[16,64,4,32]{1,0,3,2:T(8,128)(2,1)S(1)} %convert_ele, ...), kind=kLoop, calls=%fused_computation.1374 | loop fusion | bytes 1048640 | tf_op jit(solution)/shard_map/squeeze | solution.py:28
  89.2 1.5 %collective-permute-start.20 = (bf16[1,64,4,32]{1,3,2,0:T(8,128)(2,1)S(1)}, bf16[1,64,4,32]{1,3,2,0:T(8,128)(2,1)S(1)}, u32[]{:S(2)}, u32[]{:S(2)}) collective-permute-start(bf16[1,64,4,32]{1,3,2,0:T(8,128)(2,1)S(1)} %copy.318), channel_id=1, source_target_pairs={{0,4},{2,6},{4,8},{6,10},{8,12},{10,14},{12,16},{14,18},{16,20},{1... | collective-permute-start | bytes 49160 | tf_op jit(solution)/shard_map/ppermute | solution.py:29
  90.7 2.5 %collective-permute-start.21 = (bf16[1,64,4,32]{1,3,2,0:T(8,128)(2,1)S(1)}, bf16[1,64,4,32]{1,3,2,0:T(8,128)(2,1)S(1)}, u32[]{:S(2)}, u32[]{:S(2)}) collective-permute-start(bf16[1,64,4,32]{1,3,2,0:T(8,128)(2,1)S(1)} %copy.319), channel_id=1, source_target_pairs={{0,6},{2,8},{4,10},{6,12},{8,14},{10,16},{12,18},{14,20},{16,22},{... | collective-permute-start | bytes 49160 | tf_op jit(solution)/shard_map/ppermute | solution.py:29
  93.2 1.6 %collective-permute-start.22 = (bf16[1,64,4,32]{1,3,2,0:T(8,128)(2,1)S(1)}, bf16[1,64,4,32]{1,3,2,0:T(8,128)(2,1)S(1)}, u32[]{:S(2)}, u32[]{:S(2)}) collective-permute-start(bf16[1,64,4,32]{1,3,2,0:T(8,128)(2,1)S(1)} %copy.320), channel_id=1, source_target_pairs={{0,8},{2,10},{4,12},{6,14},{8,16},{10,18},{12,20},{14,22},{16,24},... | collective-permute-start | bytes 49160 | tf_op jit(solution)/shard_map/ppermute | solution.py:29
  95.5 1.4 collective-permute-start.24
  96.9 2.3 %collective-permute-start.25 = (bf16[1,64,4,32]{1,3,2,0:T(8,128)(2,1)S(1)}, bf16[1,64,4,32]{1,3,2,0:T(8,128)(2,1)S(1)}, u32[]{:S(2)}, u32[]{:S(2)}) collective-permute-start(bf16[1,64,4,32]{1,3,2,0:T(8,128)(2,1)S(1)} %copy.323), channel_id=1, source_target_pairs={{0,14},{2,16},{4,18},{6,20},{8,22},{10,24},{12,26},{14,28},{16,30}... | collective-permute-start | bytes 49160 | tf_op jit(solution)/shard_map/ppermute | solution.py:29
  99.2 3.4 %collective-permute-start.26 = (bf16[1,64,4,32]{1,3,2,0:T(8,128)(2,1)S(1)}, bf16[1,64,4,32]{1,3,2,0:T(8,128)(2,1)S(1)}, u32[]{:S(2)}, u32[]{:S(2)}) collective-permute-start(bf16[1,64,4,32]{1,3,2,0:T(8,128)(2,1)S(1)} %copy.324), channel_id=1, source_target_pairs={{0,16},{2,18},{4,20},{6,22},{8,24},{10,26},{12,28},{14,30},{16,0},... | collective-permute-start | bytes 49160 | tf_op jit(solution)/shard_map/ppermute | solution.py:29
  102.8 1.3 collective-permute-start.28
  104.1 2.5 %collective-permute-start.29 = (bf16[1,64,4,32]{1,3,2,0:T(8,128)(2,1)S(1)}, bf16[1,64,4,32]{1,3,2,0:T(8,128)(2,1)S(1)}, u32[]{:S(2)}, u32[]{:S(2)}) collective-permute-start(bf16[1,64,4,32]{1,3,2,0:T(8,128)(2,1)S(1)} %copy.327), channel_id=1, source_target_pairs={{0,22},{2,24},{4,26},{6,28},{8,30},{10,0},{12,2},{14,4},{16,6},{18... | collective-permute-start | bytes 49160 | tf_op jit(solution)/shard_map/ppermute | solution.py:29
  106.6 1.4 collective-permute-start.30
  108.1 2.1 %collective-permute-start.32 = (bf16[1,64,4,32]{1,3,2,0:T(8,128)(2,1)S(1)}, bf16[1,64,4,32]{1,3,2,0:T(8,128)(2,1)S(1)}, u32[]{:S(2)}, u32[]{:S(2)}) collective-permute-start(bf16[1,64,4,32]{1,3,2,0:T(8,128)(2,1)S(1)} %copy.330), channel_id=1, source_target_pairs={{0,28},{2,30},{4,0},{6,2},{8,4},{10,6},{12,8},{14,10},{16,12},{18,... | collective-permute-start | bytes 49160 | tf_op jit(solution)/shard_map/ppermute | solution.py:29
  110.2 2.1 %collective-permute-start.33 = (bf16[1,64,4,32]{1,3,2,0:T(8,128)(2,1)S(1)}, bf16[1,64,4,32]{1,3,2,0:T(8,128)(2,1)S(1)}, u32[]{:S(2)}, u32[]{:S(2)}) collective-permute-start(bf16[1,64,4,32]{1,3,2,0:T(8,128)(2,1)S(1)} %copy.331), channel_id=1, source_target_pairs={{0,30},{2,0},{4,2},{6,4},{8,6},{10,8},{12,10},{14,12},{16,14},{18,... | collective-permute-start | bytes 49160 | tf_op jit(solution)/shard_map/ppermute | solution.py:29
  113.1 1.5 collective-permute-start.4
  115.0 2.6 %collective-permute-start.6 = (bf16[1,64,4,32]{1,3,2,0:T(8,128)(2,1)S(1)}, bf16[1,64,4,32]{1,3,2,0:T(8,128)(2,1)S(1)}, u32[]{:S(2)}, u32[]{:S(2)}) collective-permute-start(bf16[1,64,4,32]{1,3,2,0:T(8,128)(2,1)S(1)} %copy.291), channel_id=1, source_target_pairs={{0,10},{2,12},{4,14},{6,16},{8,18},{10,20},{12,22},{14,24},{16,26}... | collective-permute-start | bytes 49160 | tf_op jit(solution)/shard_map/ppermute | solution.py:29
  119.0 1.9 %collective-permute-start.7 = (bf16[1,64,4,32]{1,3,2,0:T(8,128)(2,1)S(1)}, bf16[1,64,4,32]{1,3,2,0:T(8,128)(2,1)S(1)}, u32[]{:S(2)}, u32[]{:S(2)}) collective-permute-start(bf16[1,64,4,32]{1,3,2,0:T(8,128)(2,1)S(1)} %copy.292), channel_id=1, source_target_pairs={{0,12},{2,14},{4,16},{6,18},{8,20},{10,22},{12,24},{14,26},{16,28}... | collective-permute-start | bytes 49160 | tf_op jit(solution)/shard_map/ppermute | solution.py:29
  120.9 3.2 %collective-permute-start.8 = (bf16[1,64,4,32]{1,3,2,0:T(8,128)(2,1)S(1)}, bf16[1,64,4,32]{1,3,2,0:T(8,128)(2,1)S(1)}, u32[]{:S(2)}, u32[]{:S(2)}) collective-permute-start(bf16[1,64,4,32]{1,3,2,0:T(8,128)(2,1)S(1)} %copy.293), channel_id=1, source_target_pairs={{0,14},{2,16},{4,18},{6,20},{8,22},{10,24},{12,26},{14,28},{16,30}... | collective-permute-start | bytes 49160 | tf_op jit(solution)/shard_map/ppermute | solution.py:29
  124.1 1.9 %collective-permute-start.9 = (bf16[1,64,4,32]{1,3,2,0:T(8,128)(2,1)S(1)}, bf16[1,64,4,32]{1,3,2,0:T(8,128)(2,1)S(1)}, u32[]{:S(2)}, u32[]{:S(2)}) collective-permute-start(bf16[1,64,4,32]{1,3,2,0:T(8,128)(2,1)S(1)} %copy.294), channel_id=1, source_target_pairs={{0,16},{2,18},{4,20},{6,22},{8,24},{10,26},{12,28},{14,30},{16,0},... | collective-permute-start | bytes 49160 | tf_op jit(solution)/shard_map/ppermute | solution.py:29
  126.1 2.1 %collective-permute-start.11 = (bf16[1,64,4,32]{1,3,2,0:T(8,128)(2,1)S(1)}, bf16[1,64,4,32]{1,3,2,0:T(8,128)(2,1)S(1)}, u32[]{:S(2)}, u32[]{:S(2)}) collective-permute-start(bf16[1,64,4,32]{1,3,2,0:T(8,128)(2,1)S(1)} %copy.296), channel_id=1, source_target_pairs={{0,20},{2,22},{4,24},{6,26},{8,28},{10,30},{12,0},{14,2},{16,4},{1... | collective-permute-start | bytes 49160 | tf_op jit(solution)/shard_map/ppermute | solution.py:29
  128.2 1.6 %collective-permute-start.12 = (bf16[1,64,4,32]{1,3,2,0:T(8,128)(2,1)S(1)}, bf16[1,64,4,32]{1,3,2,0:T(8,128)(2,1)S(1)}, u32[]{:S(2)}, u32[]{:S(2)}) collective-permute-start(bf16[1,64,4,32]{1,3,2,0:T(8,128)(2,1)S(1)} %copy.297), channel_id=1, source_target_pairs={{0,22},{2,24},{4,26},{6,28},{8,30},{10,0},{12,2},{14,4},{16,6},{18... | collective-permute-start | bytes 49160 | tf_op jit(solution)/shard_map/ppermute | solution.py:29
  129.8 2.3 %collective-permute-start.13 = (bf16[1,64,4,32]{1,3,2,0:T(8,128)(2,1)S(1)}, bf16[1,64,4,32]{1,3,2,0:T(8,128)(2,1)S(1)}, u32[]{:S(2)}, u32[]{:S(2)}) collective-permute-start(bf16[1,64,4,32]{1,3,2,0:T(8,128)(2,1)S(1)} %copy.298), channel_id=1, source_target_pairs={{0,24},{2,26},{4,28},{6,30},{8,0},{10,2},{12,4},{14,6},{16,8},{18,... | collective-permute-start | bytes 49160 | tf_op jit(solution)/shard_map/ppermute | solution.py:29
  132.2 2.4 %collective-permute-start.15 = (bf16[1,64,4,32]{1,3,2,0:T(8,128)(2,1)S(1)}, bf16[1,64,4,32]{1,3,2,0:T(8,128)(2,1)S(1)}, u32[]{:S(2)}, u32[]{:S(2)}) collective-permute-start(bf16[1,64,4,32]{1,3,2,0:T(8,128)(2,1)S(1)} %copy.300), channel_id=1, source_target_pairs={{0,28},{2,30},{4,0},{6,2},{8,4},{10,6},{12,8},{14,10},{16,12},{18,... | collective-permute-start | bytes 49160 | tf_op jit(solution)/shard_map/ppermute | solution.py:29
  135.6 1.9 %collective-permute-start.35 = (f32[16,4,32]{0,2,1:T(8,128)S(1)}, f32[16,4,32]{0,2,1:T(8,128)S(1)}, u32[]{:S(2)}, u32[]{:S(2)}) collective-permute-start(f32[16,4,32]{0,2,1:T(8,128)S(1)} %get-tuple-element.189), channel_id=1, source_target_pairs={{2,0},{4,2},{6,4},{8,6},{10,8},{12,10},{14,12},{16,14},{18,16},{20... | collective-permute-start | bytes 24584 | tf_op jit(solution)/shard_map/ppermute | solution.py:42
  137.6 2.4 %collective-permute-start.34 = (f32[16,4,32]{0,2,1:T(8,128)S(1)}, f32[16,4,32]{0,2,1:T(8,128)S(1)}, u32[]{:S(2)}, u32[]{:S(2)}) collective-permute-start(f32[16,4,32]{0,2,1:T(8,128)S(1)} %get-tuple-element.188), channel_id=1, source_target_pairs={{0,2},{2,4},{4,6},{6,8},{8,10},{10,12},{12,14},{14,16},{16,18},{18... | collective-permute-start | bytes 24584 | tf_op jit(solution)/shard_map/ppermute | solution.py:41
  141.5 4.1 %collective-permute-start.18 = (f32[16,4,32]{0,2,1:T(8,128)S(1)}, f32[16,4,32]{0,2,1:T(8,128)S(1)}, u32[]{:S(2)}, u32[]{:S(2)}) collective-permute-start(f32[16,4,32]{0,2,1:T(8,128)S(1)} %get-tuple-element.187), channel_id=1, source_target_pairs={{2,0},{4,2},{6,4},{8,6},{10,8},{12,10},{14,12},{16,14},{18,16},{20... | collective-permute-start | bytes 24584 | tf_op jit(solution)/shard_map/ppermute | solution.py:42
  145.5 1.9 %collective-permute-start.17 = (f32[16,4,32]{0,2,1:T(8,128)S(1)}, f32[16,4,32]{0,2,1:T(8,128)S(1)}, u32[]{:S(2)}, u32[]{:S(2)}) collective-permute-start(f32[16,4,32]{0,2,1:T(8,128)S(1)} %get-tuple-element.186), channel_id=1, source_target_pairs={{0,2},{2,4},{4,6},{6,8},{8,10},{10,12},{12,14},{14,16},{16,18},{18... | collective-permute-start | bytes 24584 | tf_op jit(solution)/shard_map/ppermute | solution.py:41
  148.0 4.1 %collective-permute-done.17 = f32[16,4,32]{0,2,1:T(8,128)S(1)} collective-permute-done((f32[16,4,32]{0,2,1:T(8,128)S(1)}, f32[16,4,32]{0,2,1:T(8,128)S(1)}, u32[]{:S(2)}, u32[]{:S(2)}) %collective-permute-start.17) | collective-permute-done | bytes 8224 | tf_op jit(solution)/shard_map/ppermute | solution.py:41
  (340 shorter events, 69.5 us)
Async XLA Ops:
  25.5 21.4 %collective-permute-start.1 = (bf16[4,4,16,1024]{3,2,1,0:T(8,128)(2,1)S(1)}, bf16[4,4,16,1024]{3,2,1,0:T(8,128)(2,1)S(1)}, u32[]{:S(2)}, u32[]{:S(2)}) collective-permute-start(bf16[4,4,16,1024]{3,2,1,0:T(8,128)(2,1)S(1)} %get-tuple-element.149), channel_id=1, source_target_pairs={{1,0},{3,2},{5,4},{7,6},{9,8},{11,10},{13,12},{15,14},{17,16},{19,... | collective-permute-start | bytes 1572872 | tf_op jit(solution)/shard_map/ppermute | solution.py:42
  26.8 20.1 %collective-permute-start = (bf16[4,4,16,1024]{3,2,1,0:T(8,128)(2,1)S(1)}, bf16[4,4,16,1024]{3,2,1,0:T(8,128)(2,1)S(1)}, u32[]{:S(2)}, u32[]{:S(2)}) collective-permute-start(bf16[4,4,16,1024]{3,2,1,0:T(8,128)(2,1)S(1)} %get-tuple-element.148), channel_id=1, source_target_pairs={{0,1},{2,3},{4,5},{6,7},{8,9},{10,11},{12,13},{14,15},{16,17},{18,... | collective-permute-start | bytes 1572872 | tf_op jit(solution)/shard_map/ppermute | solution.py:41
  89.1 6.5 %collective-permute-start.19 = (bf16[1,64,4,32]{1,3,2,0:T(8,128)(2,1)S(1)}, bf16[1,64,4,32]{1,3,2,0:T(8,128)(2,1)S(1)}, u32[]{:S(2)}, u32[]{:S(2)}) collective-permute-start(bf16[1,64,4,32]{1,3,2,0:T(8,128)(2,1)S(1)} %copy.317), channel_id=1, source_target_pairs={{0,2},{2,4},{4,6},{6,8},{8,10},{10,12},{12,14},{14,16},{16,18},{18... | collective-permute-start | bytes 49160 | tf_op jit(solution)/shard_map/ppermute | solution.py:29
  89.2 7.8 %collective-permute-start.20 = (bf16[1,64,4,32]{1,3,2,0:T(8,128)(2,1)S(1)}, bf16[1,64,4,32]{1,3,2,0:T(8,128)(2,1)S(1)}, u32[]{:S(2)}, u32[]{:S(2)}) collective-permute-start(bf16[1,64,4,32]{1,3,2,0:T(8,128)(2,1)S(1)} %copy.318), channel_id=1, source_target_pairs={{0,4},{2,6},{4,8},{6,10},{8,12},{10,14},{12,16},{14,18},{16,20},{1... | collective-permute-start | bytes 49160 | tf_op jit(solution)/shard_map/ppermute | solution.py:29
  90.7 8.5 %collective-permute-start.21 = (bf16[1,64,4,32]{1,3,2,0:T(8,128)(2,1)S(1)}, bf16[1,64,4,32]{1,3,2,0:T(8,128)(2,1)S(1)}, u32[]{:S(2)}, u32[]{:S(2)}) collective-permute-start(bf16[1,64,4,32]{1,3,2,0:T(8,128)(2,1)S(1)} %copy.319), channel_id=1, source_target_pairs={{0,6},{2,8},{4,10},{6,12},{8,14},{10,16},{12,18},{14,20},{16,22},{... | collective-permute-start | bytes 49160 | tf_op jit(solution)/shard_map/ppermute | solution.py:29
  93.2 9.5 %collective-permute-start.22 = (bf16[1,64,4,32]{1,3,2,0:T(8,128)(2,1)S(1)}, bf16[1,64,4,32]{1,3,2,0:T(8,128)(2,1)S(1)}, u32[]{:S(2)}, u32[]{:S(2)}) collective-permute-start(bf16[1,64,4,32]{1,3,2,0:T(8,128)(2,1)S(1)} %copy.320), channel_id=1, source_target_pairs={{0,8},{2,10},{4,12},{6,14},{8,16},{10,18},{12,20},{14,22},{16,24},... | collective-permute-start | bytes 49160 | tf_op jit(solution)/shard_map/ppermute | solution.py:29
  94.8 7.9 %collective-permute-start.23 = (bf16[1,64,4,32]{1,3,2,0:T(8,128)(2,1)S(1)}, bf16[1,64,4,32]{1,3,2,0:T(8,128)(2,1)S(1)}, u32[]{:S(2)}, u32[]{:S(2)}) collective-permute-start(bf16[1,64,4,32]{1,3,2,0:T(8,128)(2,1)S(1)} %copy.321), channel_id=1, source_target_pairs={{0,10},{2,12},{4,14},{6,16},{8,18},{10,20},{12,22},{14,24},{16,26}... | collective-permute-start | bytes 49160 | tf_op jit(solution)/shard_map/ppermute | solution.py:29
  95.5 8.6 %collective-permute-start.24 = (bf16[1,64,4,32]{1,3,2,0:T(8,128)(2,1)S(1)}, bf16[1,64,4,32]{1,3,2,0:T(8,128)(2,1)S(1)}, u32[]{:S(2)}, u32[]{:S(2)}) collective-permute-start(bf16[1,64,4,32]{1,3,2,0:T(8,128)(2,1)S(1)} %copy.322), channel_id=1, source_target_pairs={{0,12},{2,14},{4,16},{6,18},{8,20},{10,22},{12,24},{14,26},{16,28}... | collective-permute-start | bytes 49160 | tf_op jit(solution)/shard_map/ppermute | solution.py:29
  96.9 9.7 %collective-permute-start.25 = (bf16[1,64,4,32]{1,3,2,0:T(8,128)(2,1)S(1)}, bf16[1,64,4,32]{1,3,2,0:T(8,128)(2,1)S(1)}, u32[]{:S(2)}, u32[]{:S(2)}) collective-permute-start(bf16[1,64,4,32]{1,3,2,0:T(8,128)(2,1)S(1)} %copy.323), channel_id=1, source_target_pairs={{0,14},{2,16},{4,18},{6,20},{8,22},{10,24},{12,26},{14,28},{16,30}... | collective-permute-start | bytes 49160 | tf_op jit(solution)/shard_map/ppermute | solution.py:29
  99.2 8.8 %collective-permute-start.26 = (bf16[1,64,4,32]{1,3,2,0:T(8,128)(2,1)S(1)}, bf16[1,64,4,32]{1,3,2,0:T(8,128)(2,1)S(1)}, u32[]{:S(2)}, u32[]{:S(2)}) collective-permute-start(bf16[1,64,4,32]{1,3,2,0:T(8,128)(2,1)S(1)} %copy.324), channel_id=1, source_target_pairs={{0,16},{2,18},{4,20},{6,22},{8,24},{10,26},{12,28},{14,30},{16,0},... | collective-permute-start | bytes 49160 | tf_op jit(solution)/shard_map/ppermute | solution.py:29
  102.8 7.4 %collective-permute-start.28 = (bf16[1,64,4,32]{1,3,2,0:T(8,128)(2,1)S(1)}, bf16[1,64,4,32]{1,3,2,0:T(8,128)(2,1)S(1)}, u32[]{:S(2)}, u32[]{:S(2)}) collective-permute-start(bf16[1,64,4,32]{1,3,2,0:T(8,128)(2,1)S(1)} %copy.326), channel_id=1, source_target_pairs={{0,20},{2,22},{4,24},{6,26},{8,28},{10,30},{12,0},{14,2},{16,4},{1... | collective-permute-start | bytes 49160 | tf_op jit(solution)/shard_map/ppermute | solution.py:29
  104.1 8.3 %collective-permute-start.29 = (bf16[1,64,4,32]{1,3,2,0:T(8,128)(2,1)S(1)}, bf16[1,64,4,32]{1,3,2,0:T(8,128)(2,1)S(1)}, u32[]{:S(2)}, u32[]{:S(2)}) collective-permute-start(bf16[1,64,4,32]{1,3,2,0:T(8,128)(2,1)S(1)} %copy.327), channel_id=1, source_target_pairs={{0,22},{2,24},{4,26},{6,28},{8,30},{10,0},{12,2},{14,4},{16,6},{18... | collective-permute-start | bytes 49160 | tf_op jit(solution)/shard_map/ppermute | solution.py:29
  106.6 5.8 %collective-permute-start.30 = (bf16[1,64,4,32]{1,3,2,0:T(8,128)(2,1)S(1)}, bf16[1,64,4,32]{1,3,2,0:T(8,128)(2,1)S(1)}, u32[]{:S(2)}, u32[]{:S(2)}) collective-permute-start(bf16[1,64,4,32]{1,3,2,0:T(8,128)(2,1)S(1)} %copy.328), channel_id=1, source_target_pairs={{0,24},{2,26},{4,28},{6,30},{8,0},{10,2},{12,4},{14,6},{16,8},{18,... | collective-permute-start | bytes 49160 | tf_op jit(solution)/shard_map/ppermute | solution.py:29
  108.1 6.5 %collective-permute-start.32 = (bf16[1,64,4,32]{1,3,2,0:T(8,128)(2,1)S(1)}, bf16[1,64,4,32]{1,3,2,0:T(8,128)(2,1)S(1)}, u32[]{:S(2)}, u32[]{:S(2)}) collective-permute-start(bf16[1,64,4,32]{1,3,2,0:T(8,128)(2,1)S(1)} %copy.330), channel_id=1, source_target_pairs={{0,28},{2,30},{4,0},{6,2},{8,4},{10,6},{12,8},{14,10},{16,12},{18,... | collective-permute-start | bytes 49160 | tf_op jit(solution)/shard_map/ppermute | solution.py:29
  112.4 6.6 %collective-permute-start.2 = (bf16[1,64,4,32]{1,3,2,0:T(8,128)(2,1)S(1)}, bf16[1,64,4,32]{1,3,2,0:T(8,128)(2,1)S(1)}, u32[]{:S(2)}, u32[]{:S(2)}) collective-permute-start(bf16[1,64,4,32]{1,3,2,0:T(8,128)(2,1)S(1)} %copy.287), channel_id=1, source_target_pairs={{0,2},{2,4},{4,6},{6,8},{8,10},{10,12},{12,14},{14,16},{16,18},{18... | collective-permute-start | bytes 49160 | tf_op jit(solution)/shard_map/ppermute | solution.py:29
  112.5 8.5 %collective-permute-start.3 = (bf16[1,64,4,32]{1,3,2,0:T(8,128)(2,1)S(1)}, bf16[1,64,4,32]{1,3,2,0:T(8,128)(2,1)S(1)}, u32[]{:S(2)}, u32[]{:S(2)}) collective-permute-start(bf16[1,64,4,32]{1,3,2,0:T(8,128)(2,1)S(1)} %copy.288), channel_id=1, source_target_pairs={{0,4},{2,6},{4,8},{6,10},{8,12},{10,14},{12,16},{14,18},{16,20},{1... | collective-permute-start | bytes 49160 | tf_op jit(solution)/shard_map/ppermute | solution.py:29
  113.1 11.0 %collective-permute-start.4 = (bf16[1,64,4,32]{1,3,2,0:T(8,128)(2,1)S(1)}, bf16[1,64,4,32]{1,3,2,0:T(8,128)(2,1)S(1)}, u32[]{:S(2)}, u32[]{:S(2)}) collective-permute-start(bf16[1,64,4,32]{1,3,2,0:T(8,128)(2,1)S(1)} %copy.289), channel_id=1, source_target_pairs={{0,6},{2,8},{4,10},{6,12},{8,14},{10,16},{12,18},{14,20},{16,22},{... | collective-permute-start | bytes 49160 | tf_op jit(solution)/shard_map/ppermute | solution.py:29
  114.6 11.4 %collective-permute-start.5 = (bf16[1,64,4,32]{1,3,2,0:T(8,128)(2,1)S(1)}, bf16[1,64,4,32]{1,3,2,0:T(8,128)(2,1)S(1)}, u32[]{:S(2)}, u32[]{:S(2)}) collective-permute-start(bf16[1,64,4,32]{1,3,2,0:T(8,128)(2,1)S(1)} %copy.290), channel_id=1, source_target_pairs={{0,8},{2,10},{4,12},{6,14},{8,16},{10,18},{12,20},{14,22},{16,24},... | collective-permute-start | bytes 49160 | tf_op jit(solution)/shard_map/ppermute | solution.py:29
  115.0 11.1 %collective-permute-start.6 = (bf16[1,64,4,32]{1,3,2,0:T(8,128)(2,1)S(1)}, bf16[1,64,4,32]{1,3,2,0:T(8,128)(2,1)S(1)}, u32[]{:S(2)}, u32[]{:S(2)}) collective-permute-start(bf16[1,64,4,32]{1,3,2,0:T(8,128)(2,1)S(1)} %copy.291), channel_id=1, source_target_pairs={{0,10},{2,12},{4,14},{6,16},{8,18},{10,20},{12,22},{14,24},{16,26}... | collective-permute-start | bytes 49160 | tf_op jit(solution)/shard_map/ppermute | solution.py:29
  119.0 9.2 %collective-permute-start.7 = (bf16[1,64,4,32]{1,3,2,0:T(8,128)(2,1)S(1)}, bf16[1,64,4,32]{1,3,2,0:T(8,128)(2,1)S(1)}, u32[]{:S(2)}, u32[]{:S(2)}) collective-permute-start(bf16[1,64,4,32]{1,3,2,0:T(8,128)(2,1)S(1)} %copy.292), channel_id=1, source_target_pairs={{0,12},{2,14},{4,16},{6,18},{8,20},{10,22},{12,24},{14,26},{16,28}... | collective-permute-start | bytes 49160 | tf_op jit(solution)/shard_map/ppermute | solution.py:29
  120.9 8.9 %collective-permute-start.8 = (bf16[1,64,4,32]{1,3,2,0:T(8,128)(2,1)S(1)}, bf16[1,64,4,32]{1,3,2,0:T(8,128)(2,1)S(1)}, u32[]{:S(2)}, u32[]{:S(2)}) collective-permute-start(bf16[1,64,4,32]{1,3,2,0:T(8,128)(2,1)S(1)} %copy.293), channel_id=1, source_target_pairs={{0,14},{2,16},{4,18},{6,20},{8,22},{10,24},{12,26},{14,28},{16,30}... | collective-permute-start | bytes 49160 | tf_op jit(solution)/shard_map/ppermute | solution.py:29
  124.1 8.0 %collective-permute-start.9 = (bf16[1,64,4,32]{1,3,2,0:T(8,128)(2,1)S(1)}, bf16[1,64,4,32]{1,3,2,0:T(8,128)(2,1)S(1)}, u32[]{:S(2)}, u32[]{:S(2)}) collective-permute-start(bf16[1,64,4,32]{1,3,2,0:T(8,128)(2,1)S(1)} %copy.294), channel_id=1, source_target_pairs={{0,16},{2,18},{4,20},{6,22},{8,24},{10,26},{12,28},{14,30},{16,0},... | collective-permute-start | bytes 49160 | tf_op jit(solution)/shard_map/ppermute | solution.py:29
  126.0 6.2 %collective-permute-start.10 = (bf16[1,64,4,32]{1,3,2,0:T(8,128)(2,1)S(1)}, bf16[1,64,4,32]{1,3,2,0:T(8,128)(2,1)S(1)}, u32[]{:S(2)}, u32[]{:S(2)}) collective-permute-start(bf16[1,64,4,32]{1,3,2,0:T(8,128)(2,1)S(1)} %copy.295), channel_id=1, source_target_pairs={{0,18},{2,20},{4,22},{6,24},{8,26},{10,28},{12,30},{14,0},{16,2},{... | collective-permute-start | bytes 49160 | tf_op jit(solution)/shard_map/ppermute | solution.py:29
  126.1 8.5 %collective-permute-start.11 = (bf16[1,64,4,32]{1,3,2,0:T(8,128)(2,1)S(1)}, bf16[1,64,4,32]{1,3,2,0:T(8,128)(2,1)S(1)}, u32[]{:S(2)}, u32[]{:S(2)}) collective-permute-start(bf16[1,64,4,32]{1,3,2,0:T(8,128)(2,1)S(1)} %copy.296), channel_id=1, source_target_pairs={{0,20},{2,22},{4,24},{6,26},{8,28},{10,30},{12,0},{14,2},{16,4},{1... | collective-permute-start | bytes 49160 | tf_op jit(solution)/shard_map/ppermute | solution.py:29
  128.2 7.4 %collective-permute-start.12 = (bf16[1,64,4,32]{1,3,2,0:T(8,128)(2,1)S(1)}, bf16[1,64,4,32]{1,3,2,0:T(8,128)(2,1)S(1)}, u32[]{:S(2)}, u32[]{:S(2)}) collective-permute-start(bf16[1,64,4,32]{1,3,2,0:T(8,128)(2,1)S(1)} %copy.297), channel_id=1, source_target_pairs={{0,22},{2,24},{4,26},{6,28},{8,30},{10,0},{12,2},{14,4},{16,6},{18... | collective-permute-start | bytes 49160 | tf_op jit(solution)/shard_map/ppermute | solution.py:29
  129.8 7.7 %collective-permute-start.13 = (bf16[1,64,4,32]{1,3,2,0:T(8,128)(2,1)S(1)}, bf16[1,64,4,32]{1,3,2,0:T(8,128)(2,1)S(1)}, u32[]{:S(2)}, u32[]{:S(2)}) collective-permute-start(bf16[1,64,4,32]{1,3,2,0:T(8,128)(2,1)S(1)} %copy.298), channel_id=1, source_target_pairs={{0,24},{2,26},{4,28},{6,30},{8,0},{10,2},{12,4},{14,6},{16,8},{18,... | collective-permute-start | bytes 49160 | tf_op jit(solution)/shard_map/ppermute | solution.py:29
  132.1 7.8 %collective-permute-start.14 = (bf16[1,64,4,32]{1,3,2,0:T(8,128)(2,1)S(1)}, bf16[1,64,4,32]{1,3,2,0:T(8,128)(2,1)S(1)}, u32[]{:S(2)}, u32[]{:S(2)}) collective-permute-start(bf16[1,64,4,32]{1,3,2,0:T(8,128)(2,1)S(1)} %copy.299), channel_id=1, source_target_pairs={{0,26},{2,28},{4,30},{6,0},{8,2},{10,4},{12,6},{14,8},{16,10},{18,... | collective-permute-start | bytes 49160 | tf_op jit(solution)/shard_map/ppermute | solution.py:29
  132.2 7.8 %collective-permute-start.15 = (bf16[1,64,4,32]{1,3,2,0:T(8,128)(2,1)S(1)}, bf16[1,64,4,32]{1,3,2,0:T(8,128)(2,1)S(1)}, u32[]{:S(2)}, u32[]{:S(2)}) collective-permute-start(bf16[1,64,4,32]{1,3,2,0:T(8,128)(2,1)S(1)} %copy.300), channel_id=1, source_target_pairs={{0,28},{2,30},{4,0},{6,2},{8,4},{10,6},{12,8},{14,10},{16,12},{18,... | collective-permute-start | bytes 49160 | tf_op jit(solution)/shard_map/ppermute | solution.py:29
  135.6 11.9 %collective-permute-start.35 = (f32[16,4,32]{0,2,1:T(8,128)S(1)}, f32[16,4,32]{0,2,1:T(8,128)S(1)}, u32[]{:S(2)}, u32[]{:S(2)}) collective-permute-start(f32[16,4,32]{0,2,1:T(8,128)S(1)} %get-tuple-element.189), channel_id=1, source_target_pairs={{2,0},{4,2},{6,4},{8,6},{10,8},{12,10},{14,12},{16,14},{18,16},{20... | collective-permute-start | bytes 24584 | tf_op jit(solution)/shard_map/ppermute | solution.py:42
  137.6 9.9 %collective-permute-start.34 = (f32[16,4,32]{0,2,1:T(8,128)S(1)}, f32[16,4,32]{0,2,1:T(8,128)S(1)}, u32[]{:S(2)}, u32[]{:S(2)}) collective-permute-start(f32[16,4,32]{0,2,1:T(8,128)S(1)} %get-tuple-element.188), channel_id=1, source_target_pairs={{0,2},{2,4},{4,6},{6,8},{8,10},{10,12},{12,14},{14,16},{16,18},{18... | collective-permute-start | bytes 24584 | tf_op jit(solution)/shard_map/ppermute | solution.py:41
  141.5 6.5 %collective-permute-start.18 = (f32[16,4,32]{0,2,1:T(8,128)S(1)}, f32[16,4,32]{0,2,1:T(8,128)S(1)}, u32[]{:S(2)}, u32[]{:S(2)}) collective-permute-start(f32[16,4,32]{0,2,1:T(8,128)S(1)} %get-tuple-element.187), channel_id=1, source_target_pairs={{2,0},{4,2},{6,4},{8,6},{10,8},{12,10},{14,12},{16,14},{18,16},{20... | collective-permute-start | bytes 24584 | tf_op jit(solution)/shard_map/ppermute | solution.py:42
  145.5 6.5 %collective-permute-start.17 = (f32[16,4,32]{0,2,1:T(8,128)S(1)}, f32[16,4,32]{0,2,1:T(8,128)S(1)}, u32[]{:S(2)}, u32[]{:S(2)}) collective-permute-start(f32[16,4,32]{0,2,1:T(8,128)S(1)} %get-tuple-element.186), channel_id=1, source_target_pairs={{0,2},{2,4},{4,6},{6,8},{8,10},{10,12},{12,14},{14,16},{16,18},{18... | collective-permute-start | bytes 24584 | tf_op jit(solution)/shard_map/ppermute | solution.py:41
  (25 other events, 63.6 us)
